TPU v7x, 512 devices: a whole 4x8x8 slice. The times are simulated.
512 devices in a mesh: row: 32 (over x, y), col: 16 (over z, core).
Axes of the slice: x: 4, y: 8, z: 8, core: 2. Of those that a mesh axis runs over, the one named last changes fastest.
Arguments:
- window: float32 [32, 2048, 16, 256], P('row', None, 'col'), may hold values from -7 to 8, as said below
Outputs:
- factored: float32 [32, 2048, 16, 256], P('row', None, 'col')
Inputs may be any that keep to these rules, and one draw needn't show every extreme that they name: `window`: entries above the diagonal are never read. The leading 2 * 128 by 256 block (lower triangle mirrored) is positive definite, with smallest eigenvalue 1 or more.
All inputs are finite; a program needn't handle non-finite values.
Results may differ from a plain program's by a relative error of at most 0.00028.
Values sent between devices are 32-bit elements; how exact they have to be, the bound alone decides.
A program may use at most 64 MiB of HBM per device.

v0:
```python
import jax
import jax.numpy as jnp
from jax import lax
from jax.sharding import PartitionSpec as P

NB = 128


def unmix_cols(gathered, col_count):
    height = gathered.shape[0]
    width = gathered.shape[1]
    return (
        gathered.reshape(height, col_count, width // col_count)
        .transpose(0, 2, 1)
        .reshape(height, width)
    )


def solve_rows(factor, rows_in):
    return jax.scipy.linalg.solve_triangular(factor, rows_in.T, lower=True).T


def body(window):
    blocks = window[0, :, 0, :]
    local_rows = blocks.shape[0]
    local_cols = blocks.shape[1]
    row_count = lax.axis_size("row")
    col_count = lax.axis_size("col")
    row_index = lax.axis_index("row")
    col_index = lax.axis_index("col")
    tile_height = NB // row_count
    tile_width = NB // col_count
    head_rows = local_cols * col_count // row_count
    groups = row_count // col_count
    for panel_step in range(2):
        first_col = panel_step * tile_width
        after_col = first_col + tile_width
        first_row = panel_step * tile_height
        tile_piece = blocks[first_row : first_row + tile_height, first_col:after_col]
        tile_wide = lax.all_gather(tile_piece, "col", axis=1, tiled=True)
        tile_full = lax.all_gather(tile_wide, "row", axis=0, tiled=True)
        tile_full = tile_full.reshape(row_count, tile_height, NB).transpose(1, 0, 2).reshape(NB, NB)
        diag_tile = unmix_cols(tile_full, col_count)
        symmetric = jnp.tril(diag_tile) + jnp.tril(diag_tile, -1).T
        factor = jnp.tril(jnp.linalg.cholesky(symmetric))
        panel_mine = blocks[:, first_col:after_col]
        gathered = lax.all_gather(panel_mine, "col", axis=1, tiled=True)
        solved = solve_rows(factor, unmix_cols(gathered, col_count))
        diag_rows = lax.dynamic_index_in_dim(
            factor.reshape(tile_height, row_count, NB), row_index, 1, False
        )
        panel_rows = jnp.concatenate(
            [jnp.zeros((first_row, NB), jnp.float32), diag_rows, solved[first_row + tile_height :]],
            0,
        )
        own_cols = lax.dynamic_index_in_dim(
            panel_rows.reshape(local_rows, tile_width, col_count), col_index, 2, False
        )
        sending = panel_rows[:head_rows]
        all_rows = lax.all_gather(sending, "row", axis=0, tiled=True)
        picked = lax.dynamic_index_in_dim(
            all_rows.reshape(groups, col_count, head_rows, NB), col_index, 1, False
        )
        col_rows = picked.transpose(1, 0, 2).reshape(local_cols, NB)
        update = jnp.dot(panel_rows, col_rows[after_col:].T, precision=lax.Precision.HIGHEST)
        trailing = blocks[:, after_col:] - update
        blocks = jnp.concatenate([blocks[:, :first_col], own_cols, trailing], 1)
    global_rows = jnp.arange(local_rows)[:, None] * row_count + row_index
    global_cols = jnp.arange(local_cols)[None, :] * col_count + col_index
    lower_mask = global_rows >= global_cols
    result = jnp.where(lower_mask, blocks, 0.0)
    return result[None, :, None, :]


def solution(mesh):
    in_specs = (P("row", None, "col", None),)
    out_specs = P("row", None, "col", None)
    return jax.shard_map(body, mesh=mesh, in_specs=in_specs, out_specs=out_specs, check_vma=False)
```

profile of v0, /device:TPU:14, one launch (start us, length us, event | category | flops | bytes accessed | tf_op | source)
XLA Modules:
  0.0 380.1 jit_solution(15478815313496594066)
XLA Ops:
  6.5 4.6 %copy.51 = f32[1,2048,1,256]{1,3,2,0:T(8,128)S(1)} copy(f32[1,2048,1,256]{3,2,1,0:T(1,128)} %param.4) | data formatting | bytes 4194304 | tf_op args[0]
  11.1 0.6 slice.65
  11.9 23.2 %all-gather = f32[16,8,4]{1,2,0:T(4,128)S(1)} all-gather(f32[1,8,4]{1,2,0:T(4,128)S(1)} %bitcast.136), channel_id=1, replica_groups=mesh['row'=32,'col'=16] {'col'}, dimensions={0}, use_global_device_ids=true | all-gather | bytes 2176 | tf_op jit(solution)/shard_map/all_gather | solution.py:40
  35.2 48.2 %all-gather.1 = f32[32,4,128]{2,1,0:T(4,128)S(1)} all-gather(f32[1,4,128]{2,1,0:T(4,128)S(1)} %bitcast.137), channel_id=1, replica_groups=mesh['row'=32,'col'=16] {'row'}, dimensions={0}, use_global_device_ids=true | all-gather | bytes 67584 | tf_op jit(solution)/shard_map/all_gather | solution.py:41
  84.1 11.7 %cholesky.44 = f32[128,128]{1,0:T(8,128)S(1)} custom-call(f32[128,128]{1,0:T(8,128)S(1)} %fusion.8), custom_call_target="Cholesky" | custom-call | tf_op jit(solution)/shard_map/jit(cholesky)/cholesky | solution.py:45
  96.0 0.7 compare_reduce_fusion.1
  96.7 0.6 select_bitcast_fusion.1
  97.7 9.8 %custom-call.6 = f32[1,128,128]{1,2,0:T(8,128)S(1)} custom-call(f32[1,128,128]{2,1,0:T(8,128)S(1)} %copy.63), custom_call_target="InvertDiagBlocksLowerTriangular" | custom-call | tf_op jit(solution)/shard_map/jit(_solve_triangular)/triangular_solve | solution.py:20
  107.5 1.8 copy.64
  109.4 1.1 convolution_bitcast_fusion.1
  110.7 0.7 pad_maximum_fusion
  111.5 76.0 %all-gather.11.cloned.1.call-done = f32[4096,128]{0,1:T(8,128)} async-done(((f32[128,128]{0,1:T(8,128)}), f32[4096,128]{0,1:T(8,128)}) %all-gather.11.cloned.1.call-update) | async-done | bytes 2097168 | tf_op jit(solution)/shard_map/all_gather | solution.py:60
  187.6 2.0 copy.88
  189.8 1.9 convolution_subtract_fusion
  191.7 1.3 copy-done
  193.0 0.6 slice.70
  194.0 0.8 slice_bitcast_fusion
  194.9 18.1 %all-gather.2 = f32[16,8,4]{1,2,0:T(4,128)S(1)} all-gather(f32[1,8,4]{1,2,0:T(4,128)S(1)} %bitcast.138), channel_id=1, replica_groups=mesh['row'=32,'col'=16] {'col'}, dimensions={0}, use_global_device_ids=true | all-gather | bytes 2176 | tf_op jit(solution)/shard_map/all_gather | solution.py:40
  213.1 46.1 %all-gather.3 = f32[32,4,128]{2,1,0:T(4,128)S(1)} all-gather(f32[1,4,128]{2,1,0:T(4,128)S(1)} %bitcast.139), channel_id=1, replica_groups=mesh['row'=32,'col'=16] {'row'}, dimensions={0}, use_global_device_ids=true | all-gather | bytes 67584 | tf_op jit(solution)/shard_map/all_gather | solution.py:41
  259.9 11.7 %cholesky.55 = f32[128,128]{1,0:T(8,128)S(1)} custom-call(f32[128,128]{1,0:T(8,128)S(1)} %fusion.6), custom_call_target="Cholesky" | custom-call | tf_op jit(solution)/shard_map/jit(cholesky)/cholesky | solution.py:45
  271.6 0.6 compare_reduce_fusion
  272.8 9.8 %custom-call.7 = f32[1,128,128]{1,2,0:T(8,128)S(1)} custom-call(f32[1,128,128]{2,1,0:T(8,128)S(1)} %get-tuple-element.6), custom_call_target="InvertDiagBlocksLowerTriangular" | custom-call | tf_op jit(solution)/shard_map/jit(_solve_triangular)/triangular_solve | solution.py:20
  282.8 1.8 copy.77
  284.7 1.1 convolution_bitcast_fusion
  286.1 1.0 concatenate.45
  287.0 0.7 slice.73
  288.3 0.6 copy.79
  288.9 0.7 concatenate.43
  289.7 75.8 %all-gather.15.cloned.1.call-done = f32[4096,128]{0,1:T(8,128)} async-done(((f32[128,128]{0,1:T(8,128)}), f32[4096,128]{0,1:T(8,128)}) %all-gather.15.cloned.1.call-update) | async-done | bytes 2097168 | tf_op jit(solution)/shard_map/all_gather | solution.py:60
  365.5 2.1 copy.89
  368.0 1.8 fusion
  370.0 3.6 copy.82
  (69 shorter events, 5.4 us)
Async XLA Ops:
  6.5 101.0 %all-gather.9.cloned.1.call-start = ((), (), s32[]{:S(2)}) async-start(), calls=%async_computation | async-start | bytes 1114112 | tf_op jit(solution)/shard_map/all_gather | solution.py:47
  11.8 175.8 %all-gather.11.cloned.1.call-start = ((), (), s32[]{:S(2)}) async-start(), calls=%async_computation.1 | async-start | bytes 2162688 | tf_op jit(solution)/shard_map/all_gather | solution.py:60
  111.5 171.3 %all-gather.13.cloned.1.call-start = ((), (), s32[]{:S(2)}) async-start(), calls=%async_computation.2 | async-start | bytes 1114112 | tf_op jit(solution)/shard_map/all_gather | solution.py:47
  191.7 1.3 copy-start
  193.7 171.9 %all-gather.15.cloned.1.call-start = ((), (), s32[]{:S(2)}) async-start(), calls=%async_computation.3 | async-start | bytes 2162688 | tf_op jit(solution)/shard_map/all_gather | solution.py:60
  287.0 2.6 copy-start.2
  365.5 2.4 copy-start.1
  365.5 2.5 copy-start.3
Sparse Core Ops, SparseCore 0:
  11.9 46.4 all-gather.8
  111.6 75.8 all-gather.10
  193.8 41.1 all-gather.12
  287.9 77.6 all-gather.14
where the time goes:
time: 380 us
  waiting for transfers between devices  152 us (40%)
  blocking collectives  136 us (36%)
  other arithmetic  47.1 us (12%)
  local copies, waits for them, and re-layouts  25.8 us (7%)
  between operations  13.6 us (4%)
  matrix products  5.78 us (2%)
    all_gather x2, waiting for transfers between devices, body(): all_rows = lax.all_gather(sending, 'row', axis=0, tiled=True)  152 us
    all_gather x2, blocking collectives, body(): tile_full = lax.all_gather(tile_wide, 'row', axis=0, tiled=True)  94.3 us
    all_gather x2, blocking collectives, body(): tile_wide = lax.all_gather(tile_piece, 'col', axis=1, tiled=True)  41.3 us
    another operation x6, other arithmetic, body(): factor = jnp.tril(jnp.linalg.cholesky(symmetric))  24.9 us
    another operation x4, other arithmetic, solve_rows(): return jax.scipy.linalg.solve_triangular(factor, rows_in.T, lower=True).T  20.8 us
    unnamed x18, local copies, waits for them, and re-layouts  11.1 us
  transfers between devices with their start and end apart: 4, of which 2 were waited for; matrix products, arithmetic and copies ran while one was open for 13% of the time, Pallas kernels for 0%

commit v1 on v0

--- a/solution.py
+++ b/solution.py
@@ -37,7 +37,25 @@
         after_col = first_col + tile_width
         first_row = panel_step * tile_height
         tile_piece = blocks[first_row : first_row + tile_height, first_col:after_col]
-        tile_wide = lax.all_gather(tile_piece, "col", axis=1, tiled=True)
+        ways, here, step = (lax.axis_size("col"), lax.axis_index("col"), tile_piece.shape[1])
+        shape = [n * ways if d == 1 else n for d, n in enumerate(tile_piece.shape)]
+        full = lax.dynamic_update_slice_in_dim(
+            jnp.zeros(shape, tile_piece.dtype), tile_piece, here * step, axis=1
+        )
+        going_up = going_down = tile_piece
+        for far in range(1, ways // 2 + 1):
+            going_up = lax.ppermute(going_up, "col", [(d, (d + 1) % ways) for d in range(ways)])
+            full = lax.dynamic_update_slice_in_dim(
+                full, going_up, (here - far) % ways * step, axis=1
+            )
+            if 2 * far < ways:
+                going_down = lax.ppermute(
+                    going_down, "col", [(d, (d - 1) % ways) for d in range(ways)]
+                )
+                full = lax.dynamic_update_slice_in_dim(
+                    full, going_down, (here + far) % ways * step, axis=1
+                )
+        tile_wide = full
         tile_full = lax.all_gather(tile_wide, "row", axis=0, tiled=True)
         tile_full = tile_full.reshape(row_count, tile_height, NB).transpose(1, 0, 2).reshape(NB, NB)
         diag_tile = unmix_cols(tile_full, col_count)

time: 380 us -> 422 us (1.11)
  starting transfers between devices: 0.31 us -> 47.3 us
  blocking collectives: 136 us -> 94.4 us
  waiting for transfers between devices: 152 us -> 179 us
  local copies, waits for them, and re-layouts: 25.8 us -> 34 us
    ppermute x0 -> x30, starting transfers between devices: none -> 47 us  [the longest x14 46.9 us: body(): lax.ppermute(going_down, 'col', [(d, (d - 1) % ways) for d in range(ways)])]
    all_gather x2 -> x0, blocking collectives: 41.3 us -> none  [body(): tile_wide = lax.all_gather(tile_piece, 'col', axis=1, tiled=True)]
    ppermute x0 -> x30, waiting for transfers between devices: none -> 22.3 us  [the longest x16 21.3 us: body(): lax.ppermute(going_up, 'col', [(d, (d + 1) % ways) for d in range(ways)])]
    dynamic_update_slice x0 -> x32, local copies, waits for them, and re-layouts: none -> 5.86 us  [the longest x16 3.03 us: body(): lax.dynamic_update_slice_in_dim(full, going_up, (here - far) % ways * ste...]
    all_gather x2, waiting for transfers between devices: 152 us -> 157 us  [body(): all_rows = lax.all_gather(sending, 'row', axis=0, tiled=True)]
    unnamed x18 -> x14, local copies, waits for them, and re-layouts: 11.1 us -> 10 us
  transfers between devices with their start and end apart: 4 -> 34, of which waited for: 2 -> 22; matrix products, arithmetic and copies ran while one was open for 13% -> 14% of each run, Pallas kernels for 0% -> 0%
where the time goes in v1:
time: 422 us
  waiting for transfers between devices  179 us (42%)
  blocking collectives  94.4 us (22%)
  starting transfers between devices  47.3 us (11%)
  other arithmetic  47.2 us (11%)
  local copies, waits for them, and re-layouts  34 us (8%)
  between operations  13.7 us (3%)
  matrix products  5.78 us (1%)
    all_gather x2, waiting for transfers between devices, body(): all_rows = lax.all_gather(sending, 'row', axis=0, tiled=True)  157 us
    all_gather x2, blocking collectives, body(): tile_full = lax.all_gather(tile_wide, 'row', axis=0, tiled=True)  94.4 us
    ppermute x14, starting transfers between devices, body(): lax.ppermute(going_down, 'col', [(d, (d - 1) % ways) for d in range(ways)])  46.9 us
    another operation x6, other arithmetic, body(): factor = jnp.tril(jnp.linalg.cholesky(symmetric))  24.9 us
    ppermute x16, waiting for transfers between devices, body(): lax.ppermute(going_up, 'col', [(d, (d + 1) % ways) for d in range(ways)])  21.3 us
    another operation x4, other arithmetic, solve_rows(): return jax.scipy.linalg.solve_triangular(factor, rows_in.T, lower=True).T  20.9 us
    unnamed x14, local copies, waits for them, and re-layouts  10 us
  transfers between devices with their start and end apart: 34, of which 22 were waited for; matrix products, arithmetic and copies ran while one was open for 14% of the time, Pallas kernels for 0%

profile of v1, /device:TPU:14, one launch (start us, length us, event | category | flops | bytes accessed | tf_op | source)
XLA Modules:
  0.0 421.8 jit_solution(9144641120843667106)
XLA Ops:
  6.5 4.6 %copy.139 = f32[1,2048,1,256]{1,3,2,0:T(8,128)S(1)} copy(f32[1,2048,1,256]{3,2,1,0:T(1,128)} %param.4) | data formatting | bytes 4194304 | tf_op args[0]
  11.9 8.5 %collective-permute-start.1 = (f32[4,8]{0,1:T(8,128)S(1)}, f32[4,8]{0,1:T(8,128)S(1)}, u32[]{:S(2)}, u32[]{:S(2)}) collective-permute-start(f32[4,8]{0,1:T(8,128)S(1)} %slice.64), channel_id=1, source_target_pairs={{0,15},{1,0},{2,1},{3,2},{4,3},{5,4},{6,5},{7,6},{8,7},{9,8},{10,9... | collective-permute-start | bytes 392 | tf_op jit(solution)/shard_map/ppermute | solution.py:52
  22.2 2.9 collective-permute-start.3
  26.7 3.0 collective-permute-start.5
  31.2 2.9 collective-permute-start.7
  35.8 2.9 collective-permute-start.9
  40.3 2.9 collective-permute-start.11
  44.8 3.3 collective-permute-start.13
  49.7 3.5 collective-permute-done.14
  53.6 48.3 %all-gather = f32[32,4,128]{2,1,0:T(4,128)S(1)} all-gather(f32[1,4,128]{2,1,0:T(4,128)S(1)} %dynamic_update_slice.128), channel_id=1, replica_groups=mesh['row'=32,'col'=16] {'row'}, dimensions={0}, use_global_device_ids=true | all-gather | bytes 67584 | tf_op jit(solution)/shard_map/all_gather | solution.py:59
  102.5 11.7 %cholesky.44 = f32[128,128]{1,0:T(8,128)S(1)} custom-call(f32[128,128]{1,0:T(8,128)S(1)} %fusion.8), custom_call_target="Cholesky" | custom-call | tf_op jit(solution)/shard_map/jit(cholesky)/cholesky | solution.py:63
  115.8 9.8 %custom-call.6 = f32[1,128,128]{1,2,0:T(8,128)S(1)} custom-call(f32[1,128,128]{2,1,0:T(8,128)S(1)} %copy.165), custom_call_target="InvertDiagBlocksLowerTriangular" | custom-call | tf_op jit(solution)/shard_map/jit(_solve_triangular)/triangular_solve | solution.py:20
  125.9 1.8 copy.166
  129.9 78.0 %all-gather.9.cloned.1.call-done = f32[4096,128]{0,1:T(8,128)} async-done(((f32[128,128]{0,1:T(8,128)}), f32[4096,128]{0,1:T(8,128)}) %all-gather.9.cloned.1.call-update) | async-done | bytes 2097168 | tf_op jit(solution)/shard_map/all_gather | solution.py:78
  208.0 2.0 copy.204
  210.2 1.9 convolution_subtract_fusion
  215.3 3.0 collective-permute-start.16
  220.0 2.9 collective-permute-start.18
  224.6 3.0 collective-permute-start.20
  229.1 2.9 collective-permute-start.22
  233.6 2.9 collective-permute-start.24
  238.2 3.0 collective-permute-start.26
  242.7 2.9 collective-permute-start.28
  247.3 3.8 collective-permute-done.29
  251.4 46.1 %all-gather.1 = f32[32,4,128]{2,1,0:T(4,128)S(1)} all-gather(f32[1,4,128]{2,1,0:T(4,128)S(1)} %dynamic_update_slice.129), channel_id=1, replica_groups=mesh['row'=32,'col'=16] {'row'}, dimensions={0}, use_global_device_ids=true | all-gather | bytes 67584 | tf_op jit(solution)/shard_map/all_gather | solution.py:59
  298.2 11.7 %cholesky.55 = f32[128,128]{1,0:T(8,128)S(1)} custom-call(f32[128,128]{1,0:T(8,128)S(1)} %fusion.6), custom_call_target="Cholesky" | custom-call | tf_op jit(solution)/shard_map/jit(cholesky)/cholesky | solution.py:63
  311.3 9.8 %custom-call.7 = f32[1,128,128]{1,2,0:T(8,128)S(1)} custom-call(f32[1,128,128]{2,1,0:T(8,128)S(1)} %get-tuple-element.6), custom_call_target="InvertDiagBlocksLowerTriangular" | custom-call | tf_op jit(solution)/shard_map/jit(_solve_triangular)/triangular_solve | solution.py:20
  321.3 1.8 copy.193
  328.2 78.9 %all-gather.13.cloned.1.call-done = f32[4096,128]{0,1:T(8,128)} async-done(((f32[128,128]{0,1:T(8,128)}), f32[4096,128]{0,1:T(8,128)}) %all-gather.13.cloned.1.call-update) | async-done | bytes 2097168 | tf_op jit(solution)/shard_map/all_gather | solution.py:78
  407.2 2.1 copy.205
  409.6 1.8 fusion
  411.6 3.6 copy.198
  (187 shorter events, 39.8 us)
Async XLA Ops:
  6.5 119.4 %all-gather.7.cloned.1.call-start = ((), (), s32[]{:S(2)}) async-start(), calls=%async_computation | async-start | bytes 1114112 | tf_op jit(solution)/shard_map/all_gather | solution.py:65
  11.8 196.2 %all-gather.9.cloned.1.call-start = ((), (), s32[]{:S(2)}) async-start(), calls=%async_computation.1 | async-start | bytes 2162688 | tf_op jit(solution)/shard_map/all_gather | solution.py:78
  11.8 9.8 %collective-permute-start = (f32[4,8]{0,1:T(8,128)S(1)}, f32[4,8]{0,1:T(8,128)S(1)}, u32[]{:S(2)}, u32[]{:S(2)}) collective-permute-start(f32[4,8]{0,1:T(8,128)S(1)} %slice.64), channel_id=1, source_target_pairs={{0,1},{1,2},{2,3},{3,4},{4,5},{5,6},{6,7},{7,8},{8,9},{9,10},{10,1... | collective-permute-start | bytes 392 | tf_op jit(solution)/shard_map/ppermute | solution.py:47
  11.9 10.0 %collective-permute-start.1 = (f32[4,8]{0,1:T(8,128)S(1)}, f32[4,8]{0,1:T(8,128)S(1)}, u32[]{:S(2)}, u32[]{:S(2)}) collective-permute-start(f32[4,8]{0,1:T(8,128)S(1)} %slice.64), channel_id=1, source_target_pairs={{0,15},{1,0},{2,1},{3,2},{4,3},{5,4},{6,5},{7,6},{8,7},{9,8},{10,9... | collective-permute-start | bytes 392 | tf_op jit(solution)/shard_map/ppermute | solution.py:52
  21.9 4.3 %collective-permute-start.2 = (f32[4,8]{0,1:T(8,128)S(1)}, f32[4,8]{0,1:T(8,128)S(1)}, u32[]{:S(2)}, u32[]{:S(2)}) collective-permute-start(f32[4,8]{0,1:T(8,128)S(1)} %collective-permute-done), channel_id=1, source_target_pairs={{0,1},{1,2},{2,3},{3,4},{4,5},{5,6},{6,7},{7,8},{8,9},{9,10},{10,1... | collective-permute-start | bytes 392 | tf_op jit(solution)/shard_map/ppermute | solution.py:47
  26.4 4.3 %collective-permute-start.4 = (f32[4,8]{0,1:T(8,128)S(1)}, f32[4,8]{0,1:T(8,128)S(1)}, u32[]{:S(2)}, u32[]{:S(2)}) collective-permute-start(f32[4,8]{0,1:T(8,128)S(1)} %collective-permute-done.2), channel_id=1, source_target_pairs={{0,1},{1,2},{2,3},{3,4},{4,5},{5,6},{6,7},{7,8},{8,9},{9,10},{10,1... | collective-permute-start | bytes 392 | tf_op jit(solution)/shard_map/ppermute | solution.py:47
  26.7 4.3 %collective-permute-start.5 = (f32[4,8]{0,1:T(8,128)S(1)}, f32[4,8]{0,1:T(8,128)S(1)}, u32[]{:S(2)}, u32[]{:S(2)}) collective-permute-start(f32[4,8]{0,1:T(8,128)S(1)} %collective-permute-done.3), channel_id=1, source_target_pairs={{0,15},{1,0},{2,1},{3,2},{4,3},{5,4},{6,5},{7,6},{8,7},{9,8},{10,9... | collective-permute-start | bytes 392 | tf_op jit(solution)/shard_map/ppermute | solution.py:52
  30.9 4.3 %collective-permute-start.6 = (f32[4,8]{0,1:T(8,128)S(1)}, f32[4,8]{0,1:T(8,128)S(1)}, u32[]{:S(2)}, u32[]{:S(2)}) collective-permute-start(f32[4,8]{0,1:T(8,128)S(1)} %collective-permute-done.4), channel_id=1, source_target_pairs={{0,1},{1,2},{2,3},{3,4},{4,5},{5,6},{6,7},{7,8},{8,9},{9,10},{10,1... | collective-permute-start | bytes 392 | tf_op jit(solution)/shard_map/ppermute | solution.py:47
  31.2 4.2 %collective-permute-start.7 = (f32[4,8]{0,1:T(8,128)S(1)}, f32[4,8]{0,1:T(8,128)S(1)}, u32[]{:S(2)}, u32[]{:S(2)}) collective-permute-start(f32[4,8]{0,1:T(8,128)S(1)} %collective-permute-done.5), channel_id=1, source_target_pairs={{0,15},{1,0},{2,1},{3,2},{4,3},{5,4},{6,5},{7,6},{8,7},{9,8},{10,9... | collective-permute-start | bytes 392 | tf_op jit(solution)/shard_map/ppermute | solution.py:52
  35.5 4.2 %collective-permute-start.8 = (f32[4,8]{0,1:T(8,128)S(1)}, f32[4,8]{0,1:T(8,128)S(1)}, u32[]{:S(2)}, u32[]{:S(2)}) collective-permute-start(f32[4,8]{0,1:T(8,128)S(1)} %collective-permute-done.6), channel_id=1, source_target_pairs={{0,1},{1,2},{2,3},{3,4},{4,5},{5,6},{6,7},{7,8},{8,9},{9,10},{10,1... | collective-permute-start | bytes 392 | tf_op jit(solution)/shard_map/ppermute | solution.py:47
  35.8 4.2 %collective-permute-start.9 = (f32[4,8]{0,1:T(8,128)S(1)}, f32[4,8]{0,1:T(8,128)S(1)}, u32[]{:S(2)}, u32[]{:S(2)}) collective-permute-start(f32[4,8]{0,1:T(8,128)S(1)} %collective-permute-done.7), channel_id=1, source_target_pairs={{0,15},{1,0},{2,1},{3,2},{4,3},{5,4},{6,5},{7,6},{8,7},{9,8},{10,9... | collective-permute-start | bytes 392 | tf_op jit(solution)/shard_map/ppermute | solution.py:52
  40.0 4.2 %collective-permute-start.10 = (f32[4,8]{0,1:T(8,128)S(1)}, f32[4,8]{0,1:T(8,128)S(1)}, u32[]{:S(2)}, u32[]{:S(2)}) collective-permute-start(f32[4,8]{0,1:T(8,128)S(1)} %collective-permute-done.8), channel_id=1, source_target_pairs={{0,1},{1,2},{2,3},{3,4},{4,5},{5,6},{6,7},{7,8},{8,9},{9,10},{10,1... | collective-permute-start | bytes 392 | tf_op jit(solution)/shard_map/ppermute | solution.py:47
  40.3 4.3 %collective-permute-start.11 = (f32[4,8]{0,1:T(8,128)S(1)}, f32[4,8]{0,1:T(8,128)S(1)}, u32[]{:S(2)}, u32[]{:S(2)}) collective-permute-start(f32[4,8]{0,1:T(8,128)S(1)} %collective-permute-done.9), channel_id=1, source_target_pairs={{0,15},{1,0},{2,1},{3,2},{4,3},{5,4},{6,5},{7,6},{8,7},{9,8},{10,9... | collective-permute-start | bytes 392 | tf_op jit(solution)/shard_map/ppermute | solution.py:52
  44.5 4.3 %collective-permute-start.12 = (f32[4,8]{0,1:T(8,128)S(1)}, f32[4,8]{0,1:T(8,128)S(1)}, u32[]{:S(2)}, u32[]{:S(2)}) collective-permute-start(f32[4,8]{0,1:T(8,128)S(1)} %collective-permute-done.10), channel_id=1, source_target_pairs={{0,1},{1,2},{2,3},{3,4},{4,5},{5,6},{6,7},{7,8},{8,9},{9,10},{10,1... | collective-permute-start | bytes 392 | tf_op jit(solution)/shard_map/ppermute | solution.py:47
  44.8 4.6 %collective-permute-start.13 = (f32[4,8]{0,1:T(8,128)S(1)}, f32[4,8]{0,1:T(8,128)S(1)}, u32[]{:S(2)}, u32[]{:S(2)}) collective-permute-start(f32[4,8]{0,1:T(8,128)S(1)} %collective-permute-done.11), channel_id=1, source_target_pairs={{0,15},{1,0},{2,1},{3,2},{4,3},{5,4},{6,5},{7,6},{8,7},{9,8},{10,9... | collective-permute-start | bytes 392 | tf_op jit(solution)/shard_map/ppermute | solution.py:52
  49.0 4.2 %collective-permute-start.14 = (f32[4,8]{0,1:T(8,128)S(1)}, f32[4,8]{0,1:T(8,128)S(1)}, u32[]{:S(2)}, u32[]{:S(2)}) collective-permute-start(f32[4,8]{0,1:T(8,128)S(1)} %collective-permute-done.12), channel_id=1, source_target_pairs={{0,1},{1,2},{2,3},{3,4},{4,5},{5,6},{6,7},{7,8},{8,9},{9,10},{10,1... | collective-permute-start | bytes 392 | tf_op jit(solution)/shard_map/ppermute | solution.py:47
  129.9 191.4 %all-gather.11.cloned.1.call-start = ((), (), s32[]{:S(2)}) async-start(), calls=%async_computation.2 | async-start | bytes 1114112 | tf_op jit(solution)/shard_map/all_gather | solution.py:65
  214.1 193.1 %all-gather.13.cloned.1.call-start = ((), (), s32[]{:S(2)}) async-start(), calls=%async_computation.3 | async-start | bytes 2162688 | tf_op jit(solution)/shard_map/all_gather | solution.py:78
  215.2 4.2 %collective-permute-start.15 = (f32[4,8]{0,1:T(8,128)S(1)}, f32[4,8]{0,1:T(8,128)S(1)}, u32[]{:S(2)}, u32[]{:S(2)}) collective-permute-start(f32[4,8]{0,1:T(8,128)S(1)} %slice.69), channel_id=1, source_target_pairs={{0,1},{1,2},{2,3},{3,4},{4,5},{5,6},{6,7},{7,8},{8,9},{9,10},{10,1... | collective-permute-start | bytes 392 | tf_op jit(solution)/shard_map/ppermute | solution.py:47
  215.3 4.4 %collective-permute-start.16 = (f32[4,8]{0,1:T(8,128)S(1)}, f32[4,8]{0,1:T(8,128)S(1)}, u32[]{:S(2)}, u32[]{:S(2)}) collective-permute-start(f32[4,8]{0,1:T(8,128)S(1)} %slice.69), channel_id=1, source_target_pairs={{0,15},{1,0},{2,1},{3,2},{4,3},{5,4},{6,5},{7,6},{8,7},{9,8},{10,9... | collective-permute-start | bytes 392 | tf_op jit(solution)/shard_map/ppermute | solution.py:52
  219.8 4.3 %collective-permute-start.17 = (f32[4,8]{0,1:T(8,128)S(1)}, f32[4,8]{0,1:T(8,128)S(1)}, u32[]{:S(2)}, u32[]{:S(2)}) collective-permute-start(f32[4,8]{0,1:T(8,128)S(1)} %collective-permute-done.15), channel_id=1, source_target_pairs={{0,1},{1,2},{2,3},{3,4},{4,5},{5,6},{6,7},{7,8},{8,9},{9,10},{10,1... | collective-permute-start | bytes 392 | tf_op jit(solution)/shard_map/ppermute | solution.py:47
  224.3 4.3 %collective-permute-start.19 = (f32[4,8]{0,1:T(8,128)S(1)}, f32[4,8]{0,1:T(8,128)S(1)}, u32[]{:S(2)}, u32[]{:S(2)}) collective-permute-start(f32[4,8]{0,1:T(8,128)S(1)} %collective-permute-done.17), channel_id=1, source_target_pairs={{0,1},{1,2},{2,3},{3,4},{4,5},{5,6},{6,7},{7,8},{8,9},{9,10},{10,1... | collective-permute-start | bytes 392 | tf_op jit(solution)/shard_map/ppermute | solution.py:47
  224.6 4.3 %collective-permute-start.20 = (f32[4,8]{0,1:T(8,128)S(1)}, f32[4,8]{0,1:T(8,128)S(1)}, u32[]{:S(2)}, u32[]{:S(2)}) collective-permute-start(f32[4,8]{0,1:T(8,128)S(1)} %collective-permute-done.18), channel_id=1, source_target_pairs={{0,15},{1,0},{2,1},{3,2},{4,3},{5,4},{6,5},{7,6},{8,7},{9,8},{10,9... | collective-permute-start | bytes 392 | tf_op jit(solution)/shard_map/ppermute | solution.py:52
  228.8 4.2 %collective-permute-start.21 = (f32[4,8]{0,1:T(8,128)S(1)}, f32[4,8]{0,1:T(8,128)S(1)}, u32[]{:S(2)}, u32[]{:S(2)}) collective-permute-start(f32[4,8]{0,1:T(8,128)S(1)} %collective-permute-done.19), channel_id=1, source_target_pairs={{0,1},{1,2},{2,3},{3,4},{4,5},{5,6},{6,7},{7,8},{8,9},{9,10},{10,1... | collective-permute-start | bytes 392 | tf_op jit(solution)/shard_map/ppermute | solution.py:47
  229.1 4.2 %collective-permute-start.22 = (f32[4,8]{0,1:T(8,128)S(1)}, f32[4,8]{0,1:T(8,128)S(1)}, u32[]{:S(2)}, u32[]{:S(2)}) collective-permute-start(f32[4,8]{0,1:T(8,128)S(1)} %collective-permute-done.20), channel_id=1, source_target_pairs={{0,15},{1,0},{2,1},{3,2},{4,3},{5,4},{6,5},{7,6},{8,7},{9,8},{10,9... | collective-permute-start | bytes 392 | tf_op jit(solution)/shard_map/ppermute | solution.py:52
  233.3 4.2 %collective-permute-start.23 = (f32[4,8]{0,1:T(8,128)S(1)}, f32[4,8]{0,1:T(8,128)S(1)}, u32[]{:S(2)}, u32[]{:S(2)}) collective-permute-start(f32[4,8]{0,1:T(8,128)S(1)} %collective-permute-done.21), channel_id=1, source_target_pairs={{0,1},{1,2},{2,3},{3,4},{4,5},{5,6},{6,7},{7,8},{8,9},{9,10},{10,1... | collective-permute-start | bytes 392 | tf_op jit(solution)/shard_map/ppermute | solution.py:47
  233.6 4.2 %collective-permute-start.24 = (f32[4,8]{0,1:T(8,128)S(1)}, f32[4,8]{0,1:T(8,128)S(1)}, u32[]{:S(2)}, u32[]{:S(2)}) collective-permute-start(f32[4,8]{0,1:T(8,128)S(1)} %collective-permute-done.22), channel_id=1, source_target_pairs={{0,15},{1,0},{2,1},{3,2},{4,3},{5,4},{6,5},{7,6},{8,7},{9,8},{10,9... | collective-permute-start | bytes 392 | tf_op jit(solution)/shard_map/ppermute | solution.py:52
  237.8 4.3 %collective-permute-start.25 = (f32[4,8]{0,1:T(8,128)S(1)}, f32[4,8]{0,1:T(8,128)S(1)}, u32[]{:S(2)}, u32[]{:S(2)}) collective-permute-start(f32[4,8]{0,1:T(8,128)S(1)} %collective-permute-done.23), channel_id=1, source_target_pairs={{0,1},{1,2},{2,3},{3,4},{4,5},{5,6},{6,7},{7,8},{8,9},{9,10},{10,1... | collective-permute-start | bytes 392 | tf_op jit(solution)/shard_map/ppermute | solution.py:47
  238.2 4.3 %collective-permute-start.26 = (f32[4,8]{0,1:T(8,128)S(1)}, f32[4,8]{0,1:T(8,128)S(1)}, u32[]{:S(2)}, u32[]{:S(2)}) collective-permute-start(f32[4,8]{0,1:T(8,128)S(1)} %collective-permute-done.24), channel_id=1, source_target_pairs={{0,15},{1,0},{2,1},{3,2},{4,3},{5,4},{6,5},{7,6},{8,7},{9,8},{10,9... | collective-permute-start | bytes 392 | tf_op jit(solution)/shard_map/ppermute | solution.py:52
  242.4 4.2 %collective-permute-start.27 = (f32[4,8]{0,1:T(8,128)S(1)}, f32[4,8]{0,1:T(8,128)S(1)}, u32[]{:S(2)}, u32[]{:S(2)}) collective-permute-start(f32[4,8]{0,1:T(8,128)S(1)} %collective-permute-done.25), channel_id=1, source_target_pairs={{0,1},{1,2},{2,3},{3,4},{4,5},{5,6},{6,7},{7,8},{8,9},{9,10},{10,1... | collective-permute-start | bytes 392 | tf_op jit(solution)/shard_map/ppermute | solution.py:47
  242.7 4.3 %collective-permute-start.28 = (f32[4,8]{0,1:T(8,128)S(1)}, f32[4,8]{0,1:T(8,128)S(1)}, u32[]{:S(2)}, u32[]{:S(2)}) collective-permute-start(f32[4,8]{0,1:T(8,128)S(1)} %collective-permute-done.26), channel_id=1, source_target_pairs={{0,15},{1,0},{2,1},{3,2},{4,3},{5,4},{6,5},{7,6},{8,7},{9,8},{10,9... | collective-permute-start | bytes 392 | tf_op jit(solution)/shard_map/ppermute | solution.py:52
  246.9 4.2 %collective-permute-start.29 = (f32[4,8]{0,1:T(8,128)S(1)}, f32[4,8]{0,1:T(8,128)S(1)}, u32[]{:S(2)}, u32[]{:S(2)}) collective-permute-start(f32[4,8]{0,1:T(8,128)S(1)} %collective-permute-done.27), channel_id=1, source_target_pairs={{0,1},{1,2},{2,3},{3,4},{4,5},{5,6},{6,7},{7,8},{8,9},{9,10},{10,1... | collective-permute-start | bytes 392 | tf_op jit(solution)/shard_map/ppermute | solution.py:47
  (6 other events, 17.3 us)
Sparse Core Ops, SparseCore 0:
  11.9 46.5 all-gather.6
  130.0 77.8 all-gather.8
  214.2 41.1 all-gather.10
  326.4 80.7 all-gather.12
